TPU v7x, 128 devices: a whole 4x4x4 slice. The times are simulated.
128 devices in a mesh: grp: 4 (over z), tile: 32 (over y, x, core).
Axes of the slice: x: 4, y: 4, z: 4, core: 2. Of those that a mesh axis runs over, the one named last changes fastest.
Arguments:
- right_side: float32 [16, 32768], P(None, ('grp', 'tile')), may hold values from -6 to 6
- ridge: float32 [32768], P(('grp', 'tile')), may hold values from 1 to 4
- tiles: float32 [512, 1024, 1024], P(('grp', 'tile')), may hold values from -0.013671875 to 0.013671875
- tile_list: int32 [512, 2], P(('grp', 'tile')), may hold values from 0 to 31, as said below
Outputs:
- solution: float32 [16, 32768], P(None, ('grp', 'tile'))
- residual: float32 [16, 32768], P(None, ('grp', 'tile'))
Inputs may be any that keep to these rules, and one draw needn't show every extreme that they name: `tile_list`: each row is a pair (row block, column block) with row block >= column block; no pair appears twice; rows stand in packed row-major order (row block rising, then column block rising).
All inputs are finite; a program needn't handle non-finite values.
Results may differ from a plain program's by a relative error of at most 0.0003.
Values sent between devices are 32-bit elements; how exact they have to be, the bound alone decides.
No kernel may reach another device: no remote copies, remote signals or barrier semaphores. Data moves between devices by JAX's collectives and lax.ppermute only.
A program may use at most 64 MiB of HBM per device.

v0:
```python
import jax
import jax.numpy as jnp
from jax import lax
from jax.sharding import PartitionSpec as P

ITERS = 2


def gauss_solve(matrix, rhs):
    order = matrix.shape[0]
    for pivot in range(order):
        scale = 1.0 / matrix[pivot, pivot]
        row_new = matrix[pivot] * scale
        rhs_new = rhs[pivot] * scale
        factor = matrix[:, pivot] * (1.0 - (jnp.arange(order) == pivot).astype(matrix.dtype))
        matrix = matrix - factor[:, None] * row_new[None, :]
        rhs = rhs - factor[:, None] * rhs_new[None, :]
        matrix = matrix.at[pivot].set(row_new)
        rhs = rhs.at[pivot].set(rhs_new)
    return rhs


def gram(left, right):
    return lax.dot_general(
        left,
        right,
        (((1,), (1,)), ((), ())),
        precision=lax.Precision.HIGHEST,
        preferred_element_type=jnp.float32,
    )


def mixed(coeffs, rows):
    return jnp.dot(coeffs.T, rows, precision=lax.Precision.HIGHEST)


def tile_masks(order):
    rowid = lax.broadcasted_iota(jnp.int32, (order, order), 0)
    colid = lax.broadcasted_iota(jnp.int32, (order, order), 1)
    return (rowid >= colid, rowid > colid)


def apply_kernel(tiles, tile_list, field):
    order = tiles.shape[1]
    lower, strict = tile_masks(order)

    def step(total, item):
        tile, pair = item
        block_row = pair[0]
        block_col = pair[1]
        differ = block_row != block_col
        direct_tile = jnp.where(jnp.logical_or(lower, differ), tile, jnp.zeros_like(tile))
        mirror_tile = jnp.where(jnp.logical_or(strict, differ), tile, jnp.zeros_like(tile))
        row_start = block_row * order
        col_start = block_col * order
        from_col = lax.dynamic_slice_in_dim(field, col_start, order, 1)
        from_row = lax.dynamic_slice_in_dim(field, row_start, order, 1)
        into_row = lax.dot_general(
            from_col,
            direct_tile,
            (((1,), (1,)), ((), ())),
            precision=lax.Precision.HIGHEST,
            preferred_element_type=jnp.float32,
        )
        into_col = jnp.dot(
            from_row,
            mirror_tile,
            precision=lax.Precision.HIGHEST,
            preferred_element_type=jnp.float32,
        )
        total = lax.dynamic_update_slice_in_dim(
            total, lax.dynamic_slice_in_dim(total, row_start, order, 1) + into_row, row_start, 1
        )
        total = lax.dynamic_update_slice_in_dim(
            total, lax.dynamic_slice_in_dim(total, col_start, order, 1) + into_col, col_start, 1
        )
        return (total, None)

    start = jnp.zeros(field.shape, jnp.float32)
    total, _ = lax.scan(step, start, (tiles, tile_list))
    return total


def local(right_side, ridge, tiles, tile_list):
    solution = jnp.zeros_like(right_side)
    residual = right_side
    direction = right_side
    norm_now = lax.psum(gram(residual, residual), ("grp", "tile"))
    for step in range(ITERS):
        whole_direction = lax.all_gather(direction, ("grp", "tile"), axis=1, tiled=True)
        partial_image = apply_kernel(tiles, tile_list, whole_direction)
        image = (
            lax.psum_scatter(partial_image, ("grp", "tile"), scatter_dimension=1, tiled=True)
            + ridge[None, :] * direction
        )
        curvature = lax.psum(gram(direction, image), ("grp", "tile"))
        alpha = gauss_solve(curvature, norm_now)
        solution = solution + mixed(alpha, direction)
        residual = residual - mixed(alpha, image)
        if step + 1 < ITERS:
            norm_next = lax.psum(gram(residual, residual), ("grp", "tile"))
            beta = gauss_solve(norm_now, norm_next)
            direction = residual + mixed(beta, direction)
            norm_now = norm_next
    return (solution, residual)


def solution(mesh):
    return jax.shard_map(
        local,
        mesh=mesh,
        in_specs=(
            P(None, ("grp", "tile")),
            P(("grp", "tile")),
            P(("grp", "tile"), None, None),
            P(("grp", "tile"), None),
        ),
        out_specs=(P(None, ("grp", "tile")), P(None, ("grp", "tile"))),
        check_vma=False,
    )
```

profile of v0, /device:TPU:1, one launch (start us, length us, event | category | flops | bytes accessed | tf_op | source)
XLA Modules:
  0.0 1806.4 jit_solution(17161838119397110656)
XLA Ops:
  7.2 0.7 all-gather.3.cloned.1.call-update
  7.9 71.4 %all-gather.3.cloned.1.call-done = f32[16,32768]{1,0:T(8,128)} async-done(((f32[16,256]{1,0:T(8,128)}), f32[16,32768]{1,0:T(8,128)}) %all-gather.3.cloned.1.call-update) | async-done | bytes 2097168 | tf_op jit(solution)/shard_map/all_gather | solution.py:90
  79.5 55.9 %while.115 = (s32[]{:T(128)}, f32[16,32768]{1,0:T(8,128)S(1)}, s32[4,2]{0,1:T(2,128)}, f32[16,32768]{1,0:T(8,128)}, f32[4,1024,1024]{2,1,0:T(8,128)}, /*index=5*/s32[]{:T(128)}, s32[1,1]{0,1:T(1,128)}, s32[]{:T(128)}, s32[]{:T(128)}) while((s32[]{:T(128)}, f32[16,32768]{1,0:T(8,128)S(1)}, s32[4,2]{0,1:T(2,128)}, ...), condition=%wide.region_2.3_spmd.clone, body=%wide.region_1.2_spmd.clone.sunk | while | flops 408977408 | bytes 8784118 | solution.py:80
  79.6 0.8 constant_dynamic-slice_fusion.4
  83.4 5.6 fusion.227
  89.0 4.5 fusion.228
  93.5 0.8 constant_dynamic-slice_fusion.4
  97.3 5.6 fusion.227
  103.0 4.5 fusion.228
  107.5 0.8 constant_dynamic-slice_fusion.4
  111.3 5.6 fusion.227
  116.9 4.5 fusion.228
  121.4 0.8 constant_dynamic-slice_fusion.4
  125.3 5.6 fusion.227
  130.9 4.5 fusion.228
  135.4 1.3 copy-done.1
  137.0 630.1 %reduce-scatter.3.cloned.1.call-done = f32[16,256]{1,0:T(8,128)} async-done(((f32[16,32768]{1,0:T(8,128)}), f32[16,256]{1,0:T(8,128)}) %reduce-scatter.3.cloned.1.call-update) | async-done | bytes 16400 | tf_op jit(solution)/shard_map/reduce_scatter | solution.py:93
  767.0 0.9 convolution_bitcast_fusion
  767.9 69.3 %all-reduce = (f32[16,16]{1,0:T(8,128)S(1)}, f32[16,16]{1,0:T(8,128)S(1)}) all-reduce(f32[16,16]{1,0:T(8,128)S(1)} %fusion.107, f32[16,16]{1,0:T(8,128)S(1)} %convolution_bitcast_fusion), channel_id=1, replica_groups=mesh['grp'=4,'tile'=32] {'grp','tile'}, use_global_device_ids=true, to_apply=%region_0.0 | all-reduce | flops 512 | bytes 4096 | tf_op jit(solution)/shard_map/psum | solution.py:88
  848.0 0.6 slice.2191
  854.6 0.6 slice.2207
  857.9 0.6 slice.2215
  859.5 0.6 slice.2219
  864.5 0.9 convolution_subtract_fusion.1
  865.5 62.7 %psum.30 = f32[16,16]{1,0:T(8,128)S(1)} all-reduce(f32[16,16]{1,0:T(8,128)S(1)} %fusion.109), channel_id=1, replica_groups=mesh['grp'=4,'tile'=32] {'grp','tile'}, use_global_device_ids=true, to_apply=%region_5.6 | all-reduce | flops 256 | bytes 2048 | tf_op jit(solution)/shard_map/psum | solution.py:101
  931.6 0.6 slice.2241
  936.5 0.6 slice.2253
  941.6 0.6 slice.2265
  946.5 0.6 slice.2277
  949.8 0.6 slice.2285
  951.5 0.6 slice.2289
  953.1 0.8 convolution_add_fusion.1
  954.0 62.6 %all-gather.5.cloned.1.call-done = f32[16,32768]{1,0:T(8,128)} async-done(((f32[16,256]{1,0:T(8,128)}), f32[16,32768]{1,0:T(8,128)}) %all-gather.5.cloned.1.call-update) | async-done | bytes 2097168 | tf_op jit(solution)/shard_map/all_gather | solution.py:90
  1016.8 52.9 %while.116 = (s32[]{:T(128)}, f32[16,32768]{1,0:T(8,128)S(1)}, s32[4,2]{0,1:T(2,128)S(1)}, f32[16,32768]{1,0:T(8,128)}, f32[4,1024,1024]{2,1,0:T(8,128)}, /*inde...) while((s32[]{:T(128)}, f32[16,32768]{1,0:T(8,128)S(1)}, s32[4,2]{0,1:T(2,128)S(1)}, ...), condition=%wide.region_7.8_spmd.clone, body=%wide.region_6.7_spmd.clone.sunk | while | flops 408977408 | bytes 8784118 | solution.py:80
  1019.9 5.6 fusion.232
  1025.5 4.5 fusion.233
  1033.1 5.6 fusion.232
  1038.7 4.5 fusion.233
  1046.3 5.6 fusion.232
  1052.0 4.5 fusion.233
  1059.6 5.6 fusion.232
  1065.2 4.5 fusion.233
  1069.7 1.3 copy-done
  1071.3 630.1 %reduce-scatter.5.cloned.1.call-done = f32[16,256]{1,0:T(8,128)} async-done(((f32[16,32768]{1,0:T(8,128)}), f32[16,256]{1,0:T(8,128)}) %reduce-scatter.5.cloned.1.call-update) | async-done | bytes 16400 | tf_op jit(solution)/shard_map/reduce_scatter | solution.py:93
  1701.4 0.8 fusion.52
  1702.2 69.2 %psum.31 = f32[16,16]{1,0:T(8,128)S(1)} all-reduce(f32[16,16]{1,0:T(8,128)S(1)} %fusion.52), channel_id=1, replica_groups=mesh['grp'=4,'tile'=32] {'grp','tile'}, use_global_device_ids=true, to_apply=%region_9.10 | all-reduce | flops 256 | bytes 2048 | tf_op jit(solution)/shard_map/psum | solution.py:96
  1797.6 0.8 convolution_add_fusion
  1798.4 1.5 convolution_subtract_fusion
  (441 shorter events, 43.6 us)
Async XLA Ops:
  7.2 72.2 %all-gather.3.cloned.1.call-start = ((), (), s32[]{:S(2)}) async-start(), calls=%async_computation.2 | async-start | bytes 2113536 | tf_op jit(solution)/shard_map/all_gather | solution.py:90
  7.9 759.1 %reduce-scatter.3.cloned.1.call-start = ((), (), s32[]{:S(2)}) async-start(), calls=%async_computation.3 | async-start | bytes 2113536 | tf_op jit(solution)/shard_map/reduce_scatter | solution.py:93
  79.5 57.3 %copy-start.2 = (f32[16,256]{1,0:T(8,128)S(1)}, f32[16,256]{1,0:T(8,128)}, u32[]{:S(2)}) copy-start(f32[16,256]{1,0:T(8,128)} %param.194) | copy-start | bytes 49156
  79.5 687.5 %copy-start.5 = (f32[256]{0:T(256)S(1)}, f32[256]{0:T(256)}, u32[]{:S(2)}) copy-start(f32[256]{0:T(256)} %param.195) | copy-start | bytes 3076
  135.4 1.4 copy-start.1
  135.4 881.3 %copy-start.4 = (s32[4,2]{0,1:T(2,128)S(1)}, s32[4,2]{0,1:T(2,128)}, u32[]{:S(2)}) copy-start(s32[4,2]{0,1:T(2,128)} %get-tuple-element.1476) | copy-start | bytes 100
  136.8 879.8 %all-gather.5.cloned.1.call-start = ((), (), s32[]{:S(2)}) async-start(), calls=%async_computation.4 | async-start | bytes 2113536 | tf_op jit(solution)/shard_map/all_gather | solution.py:90
  953.9 747.5 %reduce-scatter.5.cloned.1.call-start = ((), (), s32[]{:S(2)}) async-start(), calls=%async_computation.5 | async-start | bytes 2113536 | tf_op jit(solution)/shard_map/reduce_scatter | solution.py:93
  1016.8 684.6 %copy-start.3 = (f32[16,256]{1,0:T(8,128)S(1)}, f32[16,256]{1,0:T(8,128)}, u32[]{:S(2)}) copy-start(f32[16,256]{1,0:T(8,128)} %convolution_add_fusion.1) | copy-start | bytes 49156
  1069.7 1.4 copy-start
Sparse Core Ops, SparseCore 0:
  10.8 68.4 all-gather.2
  136.9 630.0 reduce-scatter.2
  954.1 62.5 all-gather.4
  1071.2 630.1 reduce-scatter.4
where the time goes:
time: 1810 us
  waiting for transfers between devices  1390 us (77%)
  blocking collectives  201 us (11%)
  matrix products  87.4 us (5%)
  between operations  48.2 us (3%)
  local copies, waits for them, and re-layouts  41.3 us (2%)
  loops' own time  20 us (1%)
    reduce_scatter x2, waiting for transfers between devices, local(): lax.psum_scatter(partial_image, ('grp', 'tile'), scatter_dimension=1, til...  1260 us
    all_gather x2, waiting for transfers between devices, local(): lax.all_gather(direction, ('grp', 'tile'), axis=1, tiled=True)  134 us
    psum x1, blocking collectives, local(): norm_now = lax.psum(gram(residual, residual), ('grp', 'tile'))  69.3 us
    psum x1, blocking collectives, local(): curvature = lax.psum(gram(direction, image), ('grp', 'tile'))  69.2 us
    psum x1, blocking collectives, local(): norm_next = lax.psum(gram(residual, residual), ('grp', 'tile'))  62.7 us
    dot_general x8, matrix products, step(): lax.dot_general(from_col, direct_tile, (((1,), (1,)), ((), ())), precisio...  45.1 us
  transfers between devices with their start and end apart: 4, of which 4 were waited for; matrix products, arithmetic and copies ran while one was open for 0% of the time, Pallas kernels for 0%

commit v1 on v0

--- a/solution.py
+++ b/solution.py
@@ -85,7 +85,9 @@
     solution = jnp.zeros_like(right_side)
     residual = right_side
     direction = right_side
-    norm_now = lax.psum(gram(residual, residual), ("grp", "tile"))
+    norm_now = gram(residual, residual)
+    for idx in ("tile", "grp"):
+        norm_now = lax.psum(norm_now, idx)
     for step in range(ITERS):
         whole_direction = lax.all_gather(direction, ("grp", "tile"), axis=1, tiled=True)
         partial_image = apply_kernel(tiles, tile_list, whole_direction)

time: 1810 us -> 1810 us (level)
  blocking collectives: 201 us -> 271 us
  waiting for transfers between devices: 1390 us -> 1320 us
    reduce_scatter x2, waiting for transfers between devices: 1260 us -> 1190 us  [local(): lax.psum_scatter(partial_image, ('grp', 'tile'), scatter_dimension=1, til...]
    psum x1 -> x2, blocking collectives: 69.2 us -> 138 us  [local(): curvature = lax.psum(gram(direction, image), ('grp', 'tile'))]
    psum x1 -> x2, blocking collectives: 69.3 us -> 70.4 us  [local(): norm_now = lax.psum(norm_now, idx)]
where the time goes in v1:
time: 1810 us
  waiting for transfers between devices  1320 us (73%)
  blocking collectives  271 us (15%)
  matrix products  87.4 us (5%)
  between operations  48.2 us (3%)
  local copies, waits for them, and re-layouts  41.3 us (2%)
  loops' own time  20 us (1%)
    reduce_scatter x2, waiting for transfers between devices, local(): lax.psum_scatter(partial_image, ('grp', 'tile'), scatter_dimension=1, til...  1190 us
    psum x2, blocking collectives, local(): curvature = lax.psum(gram(direction, image), ('grp', 'tile'))  138 us
    all_gather x2, waiting for transfers between devices, local(): lax.all_gather(direction, ('grp', 'tile'), axis=1, tiled=True)  134 us
    psum x2, blocking collectives, local(): norm_now = lax.psum(norm_now, idx)  70.4 us
    psum x1, blocking collectives, local(): norm_next = lax.psum(gram(residual, residual), ('grp', 'tile'))  62.7 us
    dot_general x8, matrix products, step(): lax.dot_general(from_col, direct_tile, (((1,), (1,)), ((), ())), precisio...  45.1 us
  transfers between devices with their start and end apart: 4, of which 4 were waited for; matrix products, arithmetic and copies ran while one was open for 0% of the time, Pallas kernels for 0%

profile of v1, /device:TPU:1, one launch (start us, length us, event | category | flops | bytes accessed | tf_op | source)
XLA Modules:
  0.0 1806.2 jit_solution(15185285936068943812)
XLA Ops:
  7.2 0.7 all-gather.3.cloned.1.call-update
  7.9 71.4 %all-gather.3.cloned.1.call-done = f32[16,32768]{1,0:T(8,128)} async-done(((f32[16,256]{1,0:T(8,128)}), f32[16,32768]{1,0:T(8,128)}) %all-gather.3.cloned.1.call-update) | async-done | bytes 2097168 | tf_op jit(solution)/shard_map/all_gather | solution.py:92
  79.5 55.9 %while.115 = (s32[]{:T(128)}, f32[16,32768]{1,0:T(8,128)S(1)}, s32[4,2]{0,1:T(2,128)}, f32[16,32768]{1,0:T(8,128)}, f32[4,1024,1024]{2,1,0:T(8,128)}, /*index=5*/s32[]{:T(128)}, s32[1,1]{0,1:T(1,128)}, s32[]{:T(128)}, s32[]{:T(128)}) while((s32[]{:T(128)}, f32[16,32768]{1,0:T(8,128)S(1)}, s32[4,2]{0,1:T(2,128)}, ...), condition=%wide.region_3.4_spmd.clone, body=%wide.region_2.3_spmd.clone.sunk | while | flops 408977408 | bytes 8784118 | solution.py:80
  79.6 0.8 constant_dynamic-slice_fusion.4
  83.4 5.6 fusion.226
  89.0 4.5 fusion.227
  93.5 0.8 constant_dynamic-slice_fusion.4
  97.3 5.6 fusion.226
  103.0 4.5 fusion.227
  107.5 0.8 constant_dynamic-slice_fusion.4
  111.3 5.6 fusion.226
  116.9 4.5 fusion.227
  121.4 0.8 constant_dynamic-slice_fusion.4
  125.3 5.6 fusion.226
  130.9 4.5 fusion.227
  135.4 1.3 copy-done.1
  137.0 63.3 %psum.35 = f32[16,16]{1,0:T(8,128)S(1)} all-reduce(f32[16,16]{1,0:T(8,128)S(1)} %fusion.107), channel_id=1, replica_groups=mesh['grp'=4,'tile'=32] {'tile'}, use_global_device_ids=true, to_apply=%region_0.0 | all-reduce | flops 256 | bytes 2048 | tf_op jit(solution)/shard_map/psum | solution.py:90
  200.3 7.1 psum.36
  208.7 559.7 %reduce-scatter.3.cloned.1.call-done = f32[16,256]{1,0:T(8,128)} async-done(((f32[16,32768]{1,0:T(8,128)}), f32[16,256]{1,0:T(8,128)}) %reduce-scatter.3.cloned.1.call-update) | async-done | bytes 16400 | tf_op jit(solution)/shard_map/reduce_scatter | solution.py:95
  768.4 0.9 convolution_bitcast_fusion
  769.3 69.1 %psum.37 = f32[16,16]{1,0:T(8,128)S(1)} all-reduce(f32[16,16]{1,0:T(8,128)S(1)} %convolution_bitcast_fusion), channel_id=1, replica_groups=mesh['grp'=4,'tile'=32] {'grp','tile'}, use_global_device_ids=true, to_apply=%region_5.6 | all-reduce | flops 256 | bytes 2048 | tf_op jit(solution)/shard_map/psum | solution.py:98
  849.6 0.6 slice.2195
  854.6 0.6 slice.2207
  859.5 0.6 slice.2219
  861.1 0.6 slice.2223
  864.4 0.9 convolution_subtract_fusion.1
  865.5 62.7 %psum.38 = f32[16,16]{1,0:T(8,128)S(1)} all-reduce(f32[16,16]{1,0:T(8,128)S(1)} %fusion.109), channel_id=1, replica_groups=mesh['grp'=4,'tile'=32] {'grp','tile'}, use_global_device_ids=true, to_apply=%region_6.7 | all-reduce | flops 256 | bytes 2048 | tf_op jit(solution)/shard_map/psum | solution.py:103
  941.5 0.6 slice.2265
  946.5 0.6 slice.2277
  948.1 0.6 slice.2281
  951.4 0.6 slice.2289
  953.0 0.8 convolution_add_fusion.1
  953.9 62.5 %all-gather.5.cloned.1.call-done = f32[16,32768]{1,0:T(8,128)} async-done(((f32[16,256]{1,0:T(8,128)}), f32[16,32768]{1,0:T(8,128)}) %all-gather.5.cloned.1.call-update) | async-done | bytes 2097168 | tf_op jit(solution)/shard_map/all_gather | solution.py:92
  1016.6 52.9 %while.116 = (s32[]{:T(128)}, f32[16,32768]{1,0:T(8,128)S(1)}, s32[4,2]{0,1:T(2,128)S(1)}, f32[16,32768]{1,0:T(8,128)}, f32[4,1024,1024]{2,1,0:T(8,128)}, /*inde...) while((s32[]{:T(128)}, f32[16,32768]{1,0:T(8,128)S(1)}, s32[4,2]{0,1:T(2,128)S(1)}, ...), condition=%wide.region_8.9_spmd.clone, body=%wide.region_7.8_spmd.clone.sunk | while | flops 408977408 | bytes 8784118 | solution.py:80
  1019.7 5.6 fusion.231
  1025.3 4.5 fusion.232
  1032.9 5.6 fusion.231
  1038.5 4.5 fusion.232
  1046.1 5.6 fusion.231
  1051.8 4.5 fusion.232
  1059.3 5.6 fusion.231
  1065.0 4.5 fusion.232
  1069.5 1.3 copy-done
  1071.1 630.1 %reduce-scatter.5.cloned.1.call-done = f32[16,256]{1,0:T(8,128)} async-done(((f32[16,32768]{1,0:T(8,128)}), f32[16,256]{1,0:T(8,128)}) %reduce-scatter.5.cloned.1.call-update) | async-done | bytes 16400 | tf_op jit(solution)/shard_map/reduce_scatter | solution.py:95
  1701.2 0.8 fusion.52
  1702.0 69.2 %psum.39 = f32[16,16]{1,0:T(8,128)S(1)} all-reduce(f32[16,16]{1,0:T(8,128)S(1)} %fusion.52), channel_id=1, replica_groups=mesh['grp'=4,'tile'=32] {'grp','tile'}, use_global_device_ids=true, to_apply=%region_10.11 | all-reduce | flops 256 | bytes 2048 | tf_op jit(solution)/shard_map/psum | solution.py:98
  1797.3 0.8 convolution_add_fusion
  1798.2 1.5 convolution_subtract_fusion
  (443 shorter events, 44.9 us)
Async XLA Ops:
  7.2 72.2 %all-gather.3.cloned.1.call-start = ((), (), s32[]{:S(2)}) async-start(), calls=%async_computation.2 | async-start | bytes 2113536 | tf_op jit(solution)/shard_map/all_gather | solution.py:92
  7.9 760.5 %reduce-scatter.3.cloned.1.call-start = ((), (), s32[]{:S(2)}) async-start(), calls=%async_computation.3 | async-start | bytes 2113536 | tf_op jit(solution)/shard_map/reduce_scatter | solution.py:95
  79.5 57.3 %copy-start.2 = (f32[16,256]{1,0:T(8,128)S(1)}, f32[16,256]{1,0:T(8,128)}, u32[]{:S(2)}) copy-start(f32[16,256]{1,0:T(8,128)} %param.194) | copy-start | bytes 49156
  79.5 688.9 %copy-start.5 = (f32[256]{0:T(256)S(1)}, f32[256]{0:T(256)}, u32[]{:S(2)}) copy-start(f32[256]{0:T(256)} %param.195) | copy-start | bytes 3076
  135.4 1.4 copy-start.1
  135.4 881.1 %copy-start.4 = (s32[4,2]{0,1:T(2,128)S(1)}, s32[4,2]{0,1:T(2,128)}, u32[]{:S(2)}) copy-start(s32[4,2]{0,1:T(2,128)} %get-tuple-element.1473) | copy-start | bytes 100
  136.8 879.6 %all-gather.5.cloned.1.call-start = ((), (), s32[]{:S(2)}) async-start(), calls=%async_computation.4 | async-start | bytes 2113536 | tf_op jit(solution)/shard_map/all_gather | solution.py:92
  953.9 747.3 %reduce-scatter.5.cloned.1.call-start = ((), (), s32[]{:S(2)}) async-start(), calls=%async_computation.5 | async-start | bytes 2113536 | tf_op jit(solution)/shard_map/reduce_scatter | solution.py:95
  1016.6 684.6 %copy-start.3 = (f32[16,256]{1,0:T(8,128)S(1)}, f32[16,256]{1,0:T(8,128)}, u32[]{:S(2)}) copy-start(f32[16,256]{1,0:T(8,128)} %convolution_add_fusion.1) | copy-start | bytes 49156
  1069.5 1.4 copy-start
Sparse Core Ops, SparseCore 0:
  10.8 68.4 all-gather.2
  136.9 631.4 reduce-scatter.2
  954.0 62.3 all-gather.4
  1071.0 630.1 reduce-scatter.4
